TPU v7x, 128 devices: a whole 4x4x4 slice. The times are simulated.
128 devices in a mesh: samp: 32 (over y, z, core), layer: 4 (over x).
Axes of the slice: x: 4, y: 4, z: 4, core: 2. Of those that a mesh axis runs over, the one named last changes fastest.
Arguments:
- spins: int32 [256, 256], P('samp'), may hold values 0 or 1
- activations: bfloat16 [256, 8, 256, 256], P('samp', 'layer'), may hold values from -6 to 6
- cotangents: bfloat16 [256, 8, 256, 256], P('samp', 'layer'), may hold values from -0.023925781 to 0.023925781
- offdiag: float32 [256], P('samp'), may hold values from -24 to 24
Outputs:
- weights: float32 [256], P('samp')
- update: float32 [8, 256, 256], P('layer', 'samp')
All inputs are finite; a program needn't handle non-finite values. No bound on the sum of `spins` on one device may be relied on, other than what follows from the above.
Results may differ from a plain program's by a relative error of at most 0.0029.
Values may be sent and summed in bfloat16 or wider, within the bound.
A program may use at most 64 MiB of HBM per device.

v0:
```python
import jax
import jax.numpy as jnp
from jax import lax
from jax.sharding import PartitionSpec as P

SIDE = 16
shift_ratio = 0.1
highest = lax.Precision.HIGHEST


def laid_out(parts, dim):
    parts = jnp.moveaxis(parts, 0, dim)
    dims = parts.shape
    return parts.reshape(*dims[:dim], dims[dim] * dims[dim + 1], *dims[dim + 2 :])


def copy_for_each(shard, axis):
    length = lax.axis_size(axis)
    return lax.all_to_all(
        jnp.broadcast_to(shard[None], (length, *shard.shape)), axis, 0, 0, tiled=True
    )


def gather_directly(shard, axis, dim):
    return laid_out(copy_for_each(shard, axis), dim)


def local_energy(spins, offdiag):
    zvals = (2 * spins - 1).astype(jnp.float32).reshape(spins.shape[0], SIDE, SIDE)
    bonds = zvals * jnp.roll(zvals, -1, 2) + zvals * jnp.roll(zvals, -1, 1)
    return offdiag + jnp.sum(bonds, axis=(1, 2))


def small_factor(matrix):
    order = matrix.shape[0]
    positions = lax.iota(jnp.int32, order)

    def one_column(j, carry):
        rest, lower = carry
        column = lax.dynamic_slice_in_dim(rest, j, 1, 1)[:, 0]
        pivot = jnp.sqrt(lax.dynamic_slice_in_dim(column, j, 1)[0])
        scaled = jnp.where(positions >= j, column / pivot, jnp.float32(0.0))
        lower = lax.dynamic_update_slice_in_dim(lower, scaled[:, None], j, 1)
        rest = rest - scaled[:, None] * scaled[None, :]
        return (rest, lower)

    start = (matrix, jnp.zeros_like(matrix))
    return lax.fori_loop(0, order, one_column, start)[1]


def lower_inverse(lower):
    order = lower.shape[0]
    ident = jnp.eye(order, dtype=jnp.float32)

    def one_row(i, inverse):
        lower_row = lax.dynamic_slice_in_dim(lower, i, 1, 0)
        unit_row = lax.dynamic_slice_in_dim(ident, i, 1, 0)
        diag_entry = lax.dynamic_slice_in_dim(lower_row[0], i, 1)[0]
        known = jnp.dot(lower_row, inverse, precision=highest)
        fresh = (unit_row - known) / diag_entry
        return lax.dynamic_update_slice_in_dim(inverse, fresh, i, 0)

    return lax.fori_loop(0, order, one_row, jnp.zeros_like(lower))


def blocked_solve(matrix, rhs):
    block = matrix.shape[0] // 8
    lower_tiles = {}
    inverses = []
    for k in range(8):
        diag_tile = matrix[k * block : (k + 1) * block, k * block : (k + 1) * block]
        for c in range(k):
            diag_tile = diag_tile - jnp.dot(
                lower_tiles[k, c], lower_tiles[k, c].T, precision=highest
            )
        factor = small_factor(diag_tile)
        inverse = lower_inverse(factor)
        inverses.append(inverse)
        for r in range(k + 1, 8):
            tile = matrix[r * block : (r + 1) * block, k * block : (k + 1) * block]
            for c in range(k):
                tile = tile - jnp.dot(lower_tiles[r, c], lower_tiles[k, c].T, precision=highest)
            lower_tiles[r, k] = jnp.dot(tile, inverse.T, precision=highest)
    forward = []
    for k in range(8):
        piece = rhs[k * block : (k + 1) * block]
        for c in range(k):
            piece = piece - jnp.dot(lower_tiles[k, c], forward[c], precision=highest)
        forward.append(jnp.dot(inverses[k], piece, precision=highest))
    backward = [None] * 8
    for k in range(7, -1, -1):
        piece = forward[k]
        for r in range(k + 1, 8):
            piece = piece - jnp.dot(lower_tiles[r, k].T, backward[r], precision=highest)
        backward[k] = jnp.dot(inverses[k].T, piece, precision=highest)
    return jnp.concatenate(backward)


def body(spins, activations, cotangents, offdiag):
    s_local = spins.shape[0]
    energy_local = local_energy(spins, offdiag)
    energy = gather_directly(energy_local, "samp", 0)
    total = energy.shape[0]
    eps = (energy - jnp.mean(energy)) / jnp.sqrt(jnp.float32(total))
    jac = jnp.einsum(
        "ksad,ksae->ksde", activations, cotangents, preferred_element_type=jnp.float32
    ).astype(jnp.bfloat16)
    regrouped = lax.all_to_all(jac, "samp", split_axis=2, concat_axis=0, tiled=True)
    flat = regrouped.reshape(total, -1)
    col_mean = jnp.mean(flat, axis=0, dtype=jnp.float32)
    raw_gram = jnp.dot(flat, flat.T, preferred_element_type=jnp.float32)
    row_dots = jnp.dot(flat.astype(jnp.float32), col_mean, precision=highest)
    mean_square = jnp.sum(col_mean * col_mean)
    partial_value = (raw_gram - row_dots[:, None] - row_dots[None, :] + mean_square) / total
    gram = lax.psum(partial_value, ("samp", "layer"))
    shift = shift_ratio * jnp.trace(gram) / total
    weights = blocked_solve(gram + shift * jnp.eye(total, dtype=jnp.float32), eps)
    start = lax.axis_index("samp") * s_local
    own_weights = lax.dynamic_slice_in_dim(weights, start, s_local)
    coeffs_all = weights - jnp.mean(weights)
    update = jnp.dot(coeffs_all, flat.astype(jnp.float32), precision=highest).reshape(
        regrouped.shape[1:]
    )
    return (own_weights, update)


def solution(mesh):
    placed = (
        P("samp", None),
        P("samp", "layer", None, None),
        P("samp", "layer", None, None),
        P("samp"),
    )
    return jax.shard_map(
        body,
        mesh=mesh,
        in_specs=placed,
        out_specs=(P("samp"), P("layer", "samp", None)),
        check_vma=False,
    )
```

profile of v0, /device:TPU:1, one launch (start us, length us, event | category | flops | bytes accessed | tf_op | source)
XLA Modules:
  0.0 995.8 jit_solution(18253489442866644126)
XLA Ops:
  7.2 0.9 add_convert_fusion
  8.4 0.8 multiply_reduce_fusion.1
  10.5 9.6 all-to-all-start.1
  20.1 2.4 convolution_convert_fusion
  22.5 3.5 copy.85
  25.9 1.0 all-to-all-done.1
  27.0 6.4 all-to-all-start
  34.7 27.0 %all-to-all-done = bf16[8,2,256,256]{3,1,0,2:T(2,128)(2,1)} async-done(((bf16[8,2,256,256]{3,1,0,2:T(2,128)(2,1)}), bf16[8,2,256,256]{3,1,0,2:T(2,128)(2,1)}, u32[]{:S(2)}, u32[]{:S(2)}) %all-to-all-start) | async-done | bytes 2097184 | tf_op jit(solution)/shard_map/all_to_all | solution.py:108
  61.7 2.8 convert_reduce_fusion
  64.5 4.2 copy.135
  68.8 4.2 reshape.493
  73.6 3.5 fusion.238
  77.1 2.1 fusion.52
  79.9 3.6 copy.128
  83.5 134.9 %all-reduce.2.cloned.1.call-done = f32[256,256]{1,0:T(8,128)} async-done(((f32[256,256]{1,0:T(8,128)}), f32[256,256]{1,0:T(8,128)}) %all-reduce.2.cloned.1.call-update) | async-done | bytes 262160 | tf_op jit(solution)/shard_map/psum | solution.py:115
  218.4 1.6 select_reduce_fusion
  220.6 1.0 select_add_fusion
  221.7 44.8 %while.288 = (s32[]{:T(128)}, f32[32,32]{0,1:T(8,128)S(1)}, f32[32,32]{0,1:T(8,128)S(1)}, s32[]{:T(128)}, s32[]{:T(128)}, /*index=5*/s32[]{:T(128)}) while((s32[]{:T(128)}, f32[32,32]{0,1:T(8,128)S(1)}, f32[32,32]{0,1:T(8,128)S(1)}, s32[]{:T(128)}, s32[]{:T(128)}, /*index=5*/s32[]{:T(128)}) %tuple.681), condition=%wide.region_5.6_spmd.clone, body=%wide.region_4.5_spmd.clone.sunk | while | flops 2211 | bytes 10493 | solution.py:48
  266.6 45.1 %while.280 = (s32[]{:T(128)}, f32[32,32]{1,0:T(8,128)S(1)}, f32[32,32]{1,0:T(8,128)S(1)}, f32[32,32]{1,0:T(8,128)S(1)}, s32[]{:T(128)}, /*index=5*/s32[]{:T(128)}, s32[]{:T(128)}) while((s32[]{:T(128)}, f32[32,32]{1,0:T(8,128)S(1)}, f32[32,32]{1,0:T(8,128)S(1)}, f32[32,32]{1,0:T(8,128)S(1)}, s32[]{:T(128)}, /*index=5*/s32[]{:T(128)}, ...), condition=%wide.region_7.8_spmd, body=%wide.region_6.7_spmd.sunk | while | flops 12355 | bytes 18937 | solution.py:63
  268.6 0.8 fusion.577
  270.0 0.8 fusion.577
  272.8 0.8 fusion.577
  274.2 0.8 fusion.577
  277.0 0.8 fusion.577
  279.9 0.8 fusion.577
  281.3 0.8 fusion.577
  284.1 0.8 fusion.577
  285.5 0.8 fusion.577
  288.3 0.8 fusion.577
  289.7 0.8 fusion.577
  291.1 0.8 fusion.577
  292.5 0.8 fusion.577
  295.3 0.8 fusion.577
  296.8 0.8 fusion.577
  299.6 0.8 fusion.577
  301.0 0.8 fusion.577
  303.8 0.8 fusion.577
  306.6 0.8 fusion.577
  308.0 0.8 fusion.577
  310.8 0.8 fusion.577
  318.4 45.6 %while.289 = (s32[]{:T(128)}, f32[32,32]{0,1:T(8,128)S(1)}, f32[32,32]{0,1:T(8,128)S(1)}, s32[]{:T(128)}, s32[]{:T(128)}, /*index=5*/s32[]{:T(128)}) while((s32[]{:T(128)}, f32[32,32]{0,1:T(8,128)S(1)}, f32[32,32]{0,1:T(8,128)S(1)}, s32[]{:T(128)}, s32[]{:T(128)}, /*index=5*/s32[]{:T(128)}) %tuple.687), condition=%wide.region_11.12_spmd.clone, body=%wide.region_10.11_spmd.clone.sunk | while | flops 2211 | bytes 10493 | solution.py:48
  364.0 45.1 %while.281 = (s32[]{:T(128)}, f32[32,32]{1,0:T(8,128)S(1)}, f32[32,32]{1,0:T(8,128)S(1)}, f32[32,32]{1,0:T(8,128)S(1)}, s32[]{:T(128)}, /*index=5*/s32[]{:T(128)}, s32[]{:T(128)}) while((s32[]{:T(128)}, f32[32,32]{1,0:T(8,128)S(1)}, f32[32,32]{1,0:T(8,128)S(1)}, f32[32,32]{1,0:T(8,128)S(1)}, s32[]{:T(128)}, /*index=5*/s32[]{:T(128)}, ...), condition=%wide.region_13.14_spmd, body=%wide.region_12.13_spmd.sunk | while | flops 12355 | bytes 18937 | solution.py:63
  364.6 0.8 fusion.580
  367.5 0.8 fusion.580
  368.9 0.8 fusion.580
  371.7 0.8 fusion.580
  373.1 0.8 fusion.580
  375.9 0.8 fusion.580
  377.3 0.8 fusion.580
  378.7 0.8 fusion.580
  412.9 45.5 %while.290 = (s32[]{:T(128)}, f32[32,32]{0,1:T(8,128)S(1)}, f32[32,32]{0,1:T(8,128)S(1)}, s32[]{:T(128)}, s32[]{:T(128)}, /*index=5*/s32[]{:T(128)}) while((s32[]{:T(128)}, f32[32,32]{0,1:T(8,128)S(1)}, f32[32,32]{0,1:T(8,128)S(1)}, s32[]{:T(128)}, s32[]{:T(128)}, /*index=5*/s32[]{:T(128)}) %tuple.693), condition=%wide.region_15.16_spmd.clone, body=%wide.region_14.15_spmd.clone.sunk | while | flops 2211 | bytes 10493 | solution.py:48
  458.5 45.1 %while.282 = (s32[]{:T(128)}, f32[32,32]{1,0:T(8,128)S(1)}, f32[32,32]{1,0:T(8,128)S(1)}, f32[32,32]{1,0:T(8,128)S(1)}, s32[]{:T(128)}, /*index=5*/s32[]{:T(128)}, s32[]{:T(128)}) while((s32[]{:T(128)}, f32[32,32]{1,0:T(8,128)S(1)}, f32[32,32]{1,0:T(8,128)S(1)}, f32[32,32]{1,0:T(8,128)S(1)}, s32[]{:T(128)}, /*index=5*/s32[]{:T(128)}, ...), condition=%wide.region_17.18_spmd, body=%wide.region_16.17_spmd.sunk | while | flops 12355 | bytes 18937 | solution.py:63
  507.4 45.5 %while.291 = (s32[]{:T(128)}, f32[32,32]{0,1:T(8,128)S(1)}, f32[32,32]{0,1:T(8,128)S(1)}, s32[]{:T(128)}, s32[]{:T(128)}, /*index=5*/s32[]{:T(128)}) while((s32[]{:T(128)}, f32[32,32]{0,1:T(8,128)S(1)}, f32[32,32]{0,1:T(8,128)S(1)}, s32[]{:T(128)}, s32[]{:T(128)}, /*index=5*/s32[]{:T(128)}) %tuple.699), condition=%wide.region_19.20_spmd.clone, body=%wide.region_18.19_spmd.clone.sunk | while | flops 2211 | bytes 10493 | solution.py:48
  553.0 45.1 %while.283 = (s32[]{:T(128)}, f32[32,32]{1,0:T(8,128)S(1)}, f32[32,32]{1,0:T(8,128)S(1)}, f32[32,32]{1,0:T(8,128)S(1)}, s32[]{:T(128)}, /*index=5*/s32[]{:T(128)}, s32[]{:T(128)}) while((s32[]{:T(128)}, f32[32,32]{1,0:T(8,128)S(1)}, f32[32,32]{1,0:T(8,128)S(1)}, f32[32,32]{1,0:T(8,128)S(1)}, s32[]{:T(128)}, /*index=5*/s32[]{:T(128)}, ...), condition=%wide.region_21.22_spmd, body=%wide.region_20.21_spmd.sunk | while | flops 12355 | bytes 18937 | solution.py:63
  601.6 45.5 %while.292 = (s32[]{:T(128)}, f32[32,32]{0,1:T(8,128)S(1)}, f32[32,32]{0,1:T(8,128)S(1)}, s32[]{:T(128)}, s32[]{:T(128)}, /*index=5*/s32[]{:T(128)}) while((s32[]{:T(128)}, f32[32,32]{0,1:T(8,128)S(1)}, f32[32,32]{0,1:T(8,128)S(1)}, s32[]{:T(128)}, s32[]{:T(128)}, /*index=5*/s32[]{:T(128)}) %tuple.705), condition=%wide.region_23.24_spmd.clone, body=%wide.region_22.23_spmd.clone.sunk | while | flops 2211 | bytes 10493 | solution.py:48
  647.2 45.1 %while.284 = (s32[]{:T(128)}, f32[32,32]{1,0:T(8,128)S(1)}, f32[32,32]{1,0:T(8,128)S(1)}, f32[32,32]{1,0:T(8,128)S(1)}, s32[]{:T(128)}, /*index=5*/s32[]{:T(128)}, s32[]{:T(128)}) while((s32[]{:T(128)}, f32[32,32]{1,0:T(8,128)S(1)}, f32[32,32]{1,0:T(8,128)S(1)}, f32[32,32]{1,0:T(8,128)S(1)}, s32[]{:T(128)}, /*index=5*/s32[]{:T(128)}, ...), condition=%wide.region_25.26_spmd, body=%wide.region_24.25_spmd.sunk | while | flops 12355 | bytes 18937 | solution.py:63
  695.8 45.5 %while.293 = (s32[]{:T(128)}, f32[32,32]{0,1:T(8,128)S(1)}, f32[32,32]{0,1:T(8,128)S(1)}, s32[]{:T(128)}, s32[]{:T(128)}, /*index=5*/s32[]{:T(128)}) while((s32[]{:T(128)}, f32[32,32]{0,1:T(8,128)S(1)}, f32[32,32]{0,1:T(8,128)S(1)}, s32[]{:T(128)}, s32[]{:T(128)}, /*index=5*/s32[]{:T(128)}) %tuple.711), condition=%wide.region_27.28_spmd.clone, body=%wide.region_26.27_spmd.clone.sunk | while | flops 2211 | bytes 10493 | solution.py:48
  741.4 45.1 %while.285 = (s32[]{:T(128)}, f32[32,32]{1,0:T(8,128)S(1)}, f32[32,32]{1,0:T(8,128)S(1)}, f32[32,32]{1,0:T(8,128)S(1)}, s32[]{:T(128)}, /*index=5*/s32[]{:T(128)}, s32[]{:T(128)}) while((s32[]{:T(128)}, f32[32,32]{1,0:T(8,128)S(1)}, f32[32,32]{1,0:T(8,128)S(1)}, f32[32,32]{1,0:T(8,128)S(1)}, s32[]{:T(128)}, /*index=5*/s32[]{:T(128)}, ...), condition=%wide.region_29.30_spmd, body=%wide.region_28.29_spmd.sunk | while | flops 12355 | bytes 18937 | solution.py:63
  787.8 45.5 %while.294 = (s32[]{:T(128)}, f32[32,32]{0,1:T(8,128)S(1)}, f32[32,32]{0,1:T(8,128)S(1)}, s32[]{:T(128)}, s32[]{:T(128)}, /*index=5*/s32[]{:T(128)}) while((s32[]{:T(128)}, f32[32,32]{0,1:T(8,128)S(1)}, f32[32,32]{0,1:T(8,128)S(1)}, s32[]{:T(128)}, s32[]{:T(128)}, /*index=5*/s32[]{:T(128)}) %tuple.717), condition=%wide.region_31.32_spmd.clone, body=%wide.region_30.31_spmd.clone.sunk | while | flops 2211 | bytes 10493 | solution.py:48
  833.4 45.1 %while.286 = (s32[]{:T(128)}, f32[32,32]{1,0:T(8,128)S(1)}, f32[32,32]{1,0:T(8,128)S(1)}, f32[32,32]{1,0:T(8,128)S(1)}, s32[]{:T(128)}, /*index=5*/s32[]{:T(128)}, s32[]{:T(128)}) while((s32[]{:T(128)}, f32[32,32]{1,0:T(8,128)S(1)}, f32[32,32]{1,0:T(8,128)S(1)}, f32[32,32]{1,0:T(8,128)S(1)}, s32[]{:T(128)}, /*index=5*/s32[]{:T(128)}, ...), condition=%wide.region_33.34_spmd, body=%wide.region_32.33_spmd.sunk | while | flops 12355 | bytes 18937 | solution.py:63
  879.0 45.5 %while.295 = (s32[]{:T(128)}, f32[32,32]{0,1:T(8,128)S(1)}, f32[32,32]{0,1:T(8,128)S(1)}, s32[]{:T(128)}, s32[]{:T(128)}, /*index=5*/s32[]{:T(128)}) while((s32[]{:T(128)}, f32[32,32]{0,1:T(8,128)S(1)}, f32[32,32]{0,1:T(8,128)S(1)}, s32[]{:T(128)}, s32[]{:T(128)}, /*index=5*/s32[]{:T(128)}) %tuple.723), condition=%wide.region_35.36_spmd.clone, body=%wide.region_34.35_spmd.clone.sunk | while | flops 2211 | bytes 10493 | solution.py:48
  924.6 45.1 %while.287 = (s32[]{:T(128)}, f32[32,32]{1,0:T(8,128)S(1)}, f32[32,32]{1,0:T(8,128)S(1)}, f32[32,32]{1,0:T(8,128)S(1)}, s32[]{:T(128)}, /*index=5*/s32[]{:T(128)}, s32[]{:T(128)}) while((s32[]{:T(128)}, f32[32,32]{1,0:T(8,128)S(1)}, f32[32,32]{1,0:T(8,128)S(1)}, f32[32,32]{1,0:T(8,128)S(1)}, s32[]{:T(128)}, /*index=5*/s32[]{:T(128)}, ...), condition=%wide.region_37.38_spmd, body=%wide.region_36.37_spmd.sunk | while | flops 12355 | bytes 18937 | solution.py:63
  977.4 0.8 bitcast_reduce_fusion
  985.5 2.8 fusion.48
  (2267 shorter events, 552.5 us)
Async XLA Ops:
  7.2 13.0 %copy-start = (bf16[8,2,256,256]{3,2,1,0:T(8,128)(2,1)S(1)}, bf16[8,2,256,256]{3,2,1,0:T(8,128)(2,1)}, u32[]{:S(2)}) copy-start(bf16[8,2,256,256]{3,2,1,0:T(8,128)(2,1)} %param.37) | copy-start | bytes 6291460
  10.5 16.5 %all-to-all-start.1 = ((f32[32,1,8]{2,1,0:T(1,128)}), f32[32,1,8]{2,1,0:T(1,128)S(1)}, u32[]{:S(2)}, u32[]{:S(2)}) async-start(f32[32,1,8]{2,1,0:T(1,128)} %broadcast_in_dim.126), calls=%async_computation.1 | async-start | bytes 32768 | tf_op jit(solution)/shard_map/all_to_all | solution.py:19
  27.0 34.8 %all-to-all-start = ((bf16[8,2,256,256]{3,1,0,2:T(2,128)(2,1)}), bf16[8,2,256,256]{3,1,0,2:T(2,128)(2,1)}, u32[]{:S(2)}, u32[]{:S(2)}) async-start(bf16[8,2,256,256]{3,1,0,2:T(2,128)(2,1)} %copy.85), calls=%async_computation | async-start | bytes 4194304 | tf_op jit(solution)/shard_map/all_to_all | solution.py:108
  33.4 185.0 %all-reduce.2.cloned.1.call-start = ((), (), s32[]{:S(2)}) async-start(), calls=%async_computation.2 | async-start | bytes 524288 | tf_op jit(solution)/shard_map/psum | solution.py:115
  73.6 3.5 copy-start.1
Sparse Core Ops, SparseCore 0:
  79.3 139.0 all-reduce.1
where the time goes:
time: 1000 us; the launch traced here: 996 us
  local copies, waits for them, and re-layouts  334 us (33%)
  matrix products  242 us (24%)
  loops' own time  186 us (19%)
  waiting for transfers between devices  163 us (16%)
  other arithmetic  32.5 us (3%)
  between operations  21.3 us (2%)
  starting transfers between devices  16 us (2%)
    dot_general x256, matrix products, one_row(): known = jnp.dot(lower_row, inverse, precision=highest)  200 us
    another operation x8, loops' own time, small_factor(): return lax.fori_loop(0, order, one_column, start)[1]  183 us
    dynamic_slice x256, local copies, waits for them, and re-layouts, one_column(): pivot = jnp.sqrt(lax.dynamic_slice_in_dim(column, j, 1)[0])  151 us
    dynamic_slice x256, local copies, waits for them, and re-layouts, one_row(): diag_entry = lax.dynamic_slice_in_dim(lower_row[0], i, 1)[0]  151 us
    psum x1, waiting for transfers between devices, body(): gram = lax.psum(partial_value, ('samp', 'layer'))  135 us
    all_to_all x1, waiting for transfers between devices, body(): lax.all_to_all(jac, 'samp', split_axis=2, concat_axis=0, tiled=True)  27 us
  transfers between devices with their start and end apart: 3, of which 3 were waited for; matrix products, arithmetic and copies ran while one was open for 1% of the time, Pallas kernels for 0%

commit v1 on v0

--- a/solution.py
+++ b/solution.py
@@ -1,11 +1,20 @@
+import functools
 import jax
 import jax.numpy as jnp
 from jax import lax
 from jax.sharding import PartitionSpec as P
+from jax.lax import all_gather
 
 SIDE = 16
 shift_ratio = 0.1
 highest = lax.Precision.HIGHEST
+
+
+def remake_meshes_on_mesh(x_part, mesh_name):
+    return jnp.sum(all_gather(x_part, mesh_name), 0)
+
+
+weights_raise = functools.partial(remake_meshes_on_mesh, mesh_name=("samp", "layer"))
 
 
 def laid_out(parts, dim):
@@ -112,7 +121,7 @@
     row_dots = jnp.dot(flat.astype(jnp.float32), col_mean, precision=highest)
     mean_square = jnp.sum(col_mean * col_mean)
     partial_value = (raw_gram - row_dots[:, None] - row_dots[None, :] + mean_square) / total
-    gram = lax.psum(partial_value, ("samp", "layer"))
+    gram = weights_raise(partial_value)
     shift = shift_ratio * jnp.trace(gram) / total
     weights = blocked_solve(gram + shift * jnp.eye(total, dtype=jnp.float32), eps)
     start = lax.axis_index("samp") * s_local

time: 1000 us -> 964 us (0.964)
  waiting for transfers between devices: 163 us -> 94.2 us
  blocking collectives: 0 us -> 37.5 us
  starting transfers between devices: 16 us -> 4 us
    psum x1 -> x0, waiting for transfers between devices: 135 us -> none  [body(): gram = lax.psum(partial_value, ('samp', 'layer'))]
    all_gather x0 -> x1, waiting for transfers between devices: none -> 87.3 us  [remake_meshes_on_mesh(): return jnp.sum(all_gather(x_part, mesh_name), 0)]
    all_to_all x0 -> x1, blocking collectives: none -> 37.5 us  [body(): lax.all_to_all(jac, 'samp', split_axis=2, concat_axis=0, tiled=True)]
    all_to_all x1 -> x0, waiting for transfers between devices: 27 us -> none  [body(): lax.all_to_all(jac, 'samp', split_axis=2, concat_axis=0, tiled=True)]
    reduce_sum x0 -> x1, other arithmetic: none -> 12 us  [remake_meshes_on_mesh(): return jnp.sum(all_gather(x_part, mesh_name), 0)]
  transfers between devices with their start and end apart: 3 -> 2, of which waited for: 3 -> 2; matrix products, arithmetic and copies ran while one was open for 1% -> 1% of each run, Pallas kernels for 0% -> 0%
where the time goes in v1:
time: 964 us; the launch traced here: 959 us
  local copies, waits for them, and re-layouts  333 us (35%)
  matrix products  242 us (25%)
  loops' own time  187 us (19%)
  waiting for transfers between devices  94.2 us (10%)
  other arithmetic  38.8 us (4%)
  blocking collectives  37.5 us (4%)
  between operations  21.5 us (2%)
    dot_general x256, matrix products, one_row(): known = jnp.dot(lower_row, inverse, precision=highest)  200 us
    another operation x8, loops' own time, small_factor(): return lax.fori_loop(0, order, one_column, start)[1]  184 us
    dynamic_slice x256, local copies, waits for them, and re-layouts, one_column(): pivot = jnp.sqrt(lax.dynamic_slice_in_dim(column, j, 1)[0])  151 us
    dynamic_slice x256, local copies, waits for them, and re-layouts, one_row(): diag_entry = lax.dynamic_slice_in_dim(lower_row[0], i, 1)[0]  151 us
    all_gather x1, waiting for transfers between devices, remake_meshes_on_mesh(): return jnp.sum(all_gather(x_part, mesh_name), 0)  87.3 us
    all_to_all x1, blocking collectives, body(): lax.all_to_all(jac, 'samp', split_axis=2, concat_axis=0, tiled=True)  37.5 us
  transfers between devices with their start and end apart: 2, of which 2 were waited for; matrix products, arithmetic and copies ran while one was open for 1% of the time, Pallas kernels for 0%

profile of v1, /device:TPU:1, one launch (start us, length us, event | category | flops | bytes accessed | tf_op | source)
XLA Modules:
  0.0 958.6 jit_solution(615883060011018104)
XLA Ops:
  7.2 1.5 copy-done
  8.8 2.4 convolution_convert_fusion
  11.1 2.2 copy.85
  13.3 37.5 %all_to_all.21 = bf16[8,2,256,256]{3,1,0,2:T(2,128)(2,1)S(1)} all-to-all(bf16[8,2,256,256]{3,1,0,2:T(2,128)(2,1)S(1)} %copy.85), channel_id=1, replica_groups=mesh['samp'=32,'layer'=4] {'samp'}, dimensions={2} | all-to-all | bytes 4194304 | tf_op jit(solution)/shard_map/all_to_all | solution.py:117
  50.8 2.7 copy.136
  53.5 1.2 convert_reduce_fusion
  54.7 4.2 reshape.493
  59.6 3.5 fusion.238
  63.1 2.1 fusion.52
  66.4 4.0 all-to-all-start.1
  70.3 6.8 all-to-all-done.1
  79.2 3.6 copy.129
  82.8 87.3 %all-gather.3.cloned.1.call-done = f32[32768,256]{1,0:T(8,128)} async-done(((f32[256,256]{1,0:T(8,128)}), f32[32768,256]{1,0:T(8,128)}) %all-gather.3.cloned.1.call-update) | async-done | bytes 33554448 | tf_op jit(solution)/shard_map/all_gather | solution.py:14
  170.1 12.0 %reduce_sum.98 = f32[256,256]{1,0:T(8,128)S(1)} reduce(f32[128,256,256]{2,1,0:T(8,128)} %bitcast.1120, f32[]{:T(128)} %constant.1438.clone.1), dimensions={0}, to_apply=%region_2.3 | reduce | flops 8323072 | bytes 33816580 | tf_op jit(solution)/shard_map/reduce_sum | solution.py:14
  183.5 45.5 %while.288 = (s32[]{:T(128)}, f32[32,32]{0,1:T(8,128)S(1)}, f32[32,32]{0,1:T(8,128)S(1)}, s32[]{:T(128)}, s32[]{:T(128)}, /*index=5*/s32[]{:T(128)}) while((s32[]{:T(128)}, f32[32,32]{0,1:T(8,128)S(1)}, f32[32,32]{0,1:T(8,128)S(1)}, s32[]{:T(128)}, s32[]{:T(128)}, /*index=5*/s32[]{:T(128)}) %tuple.681), condition=%wide.region_5.6_spmd.clone, body=%wide.region_4.5_spmd.clone.sunk | while | flops 2211 | bytes 10993 | solution.py:57
  229.1 45.1 %while.280 = (s32[]{:T(128)}, f32[32,32]{1,0:T(8,128)S(1)}, f32[32,32]{1,0:T(8,128)S(1)}, f32[32,32]{1,0:T(8,128)S(1)}, s32[]{:T(128)}, /*index=5*/s32[]{:T(128)}, s32[]{:T(128)}) while((s32[]{:T(128)}, f32[32,32]{1,0:T(8,128)S(1)}, f32[32,32]{1,0:T(8,128)S(1)}, f32[32,32]{1,0:T(8,128)S(1)}, s32[]{:T(128)}, /*index=5*/s32[]{:T(128)}, ...), condition=%wide.region_7.8_spmd, body=%wide.region_6.7_spmd.sunk | while | flops 12355 | bytes 19437 | solution.py:72
  231.1 0.8 fusion.577
  232.5 0.8 fusion.577
  235.3 0.8 fusion.577
  238.2 0.8 fusion.577
  239.6 0.8 fusion.577
  242.4 0.8 fusion.577
  243.8 0.8 fusion.577
  246.6 0.8 fusion.577
  248.0 0.8 fusion.577
  249.4 0.8 fusion.577
  250.8 0.8 fusion.577
  253.7 0.8 fusion.577
  255.1 0.8 fusion.577
  257.9 0.8 fusion.577
  259.3 0.8 fusion.577
  262.1 0.8 fusion.577
  264.9 0.8 fusion.577
  266.3 0.8 fusion.577
  269.2 0.8 fusion.577
  270.6 0.8 fusion.577
  273.4 0.8 fusion.577
  279.9 45.6 %while.289 = (s32[]{:T(128)}, f32[32,32]{0,1:T(8,128)S(1)}, f32[32,32]{0,1:T(8,128)S(1)}, s32[]{:T(128)}, s32[]{:T(128)}, /*index=5*/s32[]{:T(128)}) while((s32[]{:T(128)}, f32[32,32]{0,1:T(8,128)S(1)}, f32[32,32]{0,1:T(8,128)S(1)}, s32[]{:T(128)}, s32[]{:T(128)}, /*index=5*/s32[]{:T(128)}) %tuple.687), condition=%wide.region_11.12_spmd.clone, body=%wide.region_10.11_spmd.clone.sunk | while | flops 2211 | bytes 10993 | solution.py:57
  325.5 45.1 %while.281 = (s32[]{:T(128)}, f32[32,32]{1,0:T(8,128)S(1)}, f32[32,32]{1,0:T(8,128)S(1)}, f32[32,32]{1,0:T(8,128)S(1)}, s32[]{:T(128)}, /*index=5*/s32[]{:T(128)}, s32[]{:T(128)}) while((s32[]{:T(128)}, f32[32,32]{1,0:T(8,128)S(1)}, f32[32,32]{1,0:T(8,128)S(1)}, f32[32,32]{1,0:T(8,128)S(1)}, s32[]{:T(128)}, /*index=5*/s32[]{:T(128)}, ...), condition=%wide.region_13.14_spmd, body=%wide.region_12.13_spmd.sunk | while | flops 12355 | bytes 19437 | solution.py:72
  326.1 0.8 fusion.580
  327.5 0.8 fusion.580
  330.3 0.8 fusion.580
  331.8 0.8 fusion.580
  334.6 0.8 fusion.580
  336.0 0.8 fusion.580
  337.4 0.8 fusion.580
  338.8 0.8 fusion.580
  341.6 0.8 fusion.580
  343.0 0.8 fusion.580
  371.8 45.5 %while.290 = (s32[]{:T(128)}, f32[32,32]{0,1:T(8,128)S(1)}, f32[32,32]{0,1:T(8,128)S(1)}, s32[]{:T(128)}, s32[]{:T(128)}, /*index=5*/s32[]{:T(128)}) while((s32[]{:T(128)}, f32[32,32]{0,1:T(8,128)S(1)}, f32[32,32]{0,1:T(8,128)S(1)}, s32[]{:T(128)}, s32[]{:T(128)}, /*index=5*/s32[]{:T(128)}) %tuple.693), condition=%wide.region_15.16_spmd.clone, body=%wide.region_14.15_spmd.clone.sunk | while | flops 2211 | bytes 10993 | solution.py:57
  417.4 45.1 %while.282 = (s32[]{:T(128)}, f32[32,32]{1,0:T(8,128)S(1)}, f32[32,32]{1,0:T(8,128)S(1)}, f32[32,32]{1,0:T(8,128)S(1)}, s32[]{:T(128)}, /*index=5*/s32[]{:T(128)}, s32[]{:T(128)}) while((s32[]{:T(128)}, f32[32,32]{1,0:T(8,128)S(1)}, f32[32,32]{1,0:T(8,128)S(1)}, f32[32,32]{1,0:T(8,128)S(1)}, s32[]{:T(128)}, /*index=5*/s32[]{:T(128)}, ...), condition=%wide.region_17.18_spmd, body=%wide.region_16.17_spmd.sunk | while | flops 12355 | bytes 19437 | solution.py:72
  464.4 45.5 %while.291 = (s32[]{:T(128)}, f32[32,32]{0,1:T(8,128)S(1)}, f32[32,32]{0,1:T(8,128)S(1)}, s32[]{:T(128)}, s32[]{:T(128)}, /*index=5*/s32[]{:T(128)}) while((s32[]{:T(128)}, f32[32,32]{0,1:T(8,128)S(1)}, f32[32,32]{0,1:T(8,128)S(1)}, s32[]{:T(128)}, s32[]{:T(128)}, /*index=5*/s32[]{:T(128)}) %tuple.699), condition=%wide.region_19.20_spmd.clone, body=%wide.region_18.19_spmd.clone.sunk | while | flops 2211 | bytes 10993 | solution.py:57
  510.0 45.1 %while.283 = (s32[]{:T(128)}, f32[32,32]{1,0:T(8,128)S(1)}, f32[32,32]{1,0:T(8,128)S(1)}, f32[32,32]{1,0:T(8,128)S(1)}, s32[]{:T(128)}, /*index=5*/s32[]{:T(128)}, s32[]{:T(128)}) while((s32[]{:T(128)}, f32[32,32]{1,0:T(8,128)S(1)}, f32[32,32]{1,0:T(8,128)S(1)}, f32[32,32]{1,0:T(8,128)S(1)}, s32[]{:T(128)}, /*index=5*/s32[]{:T(128)}, ...), condition=%wide.region_21.22_spmd, body=%wide.region_20.21_spmd.sunk | while | flops 12355 | bytes 19437 | solution.py:72
  557.9 45.5 %while.292 = (s32[]{:T(128)}, f32[32,32]{0,1:T(8,128)S(1)}, f32[32,32]{0,1:T(8,128)S(1)}, s32[]{:T(128)}, s32[]{:T(128)}, /*index=5*/s32[]{:T(128)}) while((s32[]{:T(128)}, f32[32,32]{0,1:T(8,128)S(1)}, f32[32,32]{0,1:T(8,128)S(1)}, s32[]{:T(128)}, s32[]{:T(128)}, /*index=5*/s32[]{:T(128)}) %tuple.705), condition=%wide.region_23.24_spmd.clone, body=%wide.region_22.23_spmd.clone.sunk | while | flops 2211 | bytes 10993 | solution.py:57
  603.5 45.1 %while.284 = (s32[]{:T(128)}, f32[32,32]{1,0:T(8,128)S(1)}, f32[32,32]{1,0:T(8,128)S(1)}, f32[32,32]{1,0:T(8,128)S(1)}, s32[]{:T(128)}, /*index=5*/s32[]{:T(128)}, s32[]{:T(128)}) while((s32[]{:T(128)}, f32[32,32]{1,0:T(8,128)S(1)}, f32[32,32]{1,0:T(8,128)S(1)}, f32[32,32]{1,0:T(8,128)S(1)}, s32[]{:T(128)}, /*index=5*/s32[]{:T(128)}, ...), condition=%wide.region_25.26_spmd, body=%wide.region_24.25_spmd.sunk | while | flops 12355 | bytes 19437 | solution.py:72
  652.6 45.5 %while.293 = (s32[]{:T(128)}, f32[32,32]{0,1:T(8,128)S(1)}, f32[32,32]{0,1:T(8,128)S(1)}, s32[]{:T(128)}, s32[]{:T(128)}, /*index=5*/s32[]{:T(128)}) while((s32[]{:T(128)}, f32[32,32]{0,1:T(8,128)S(1)}, f32[32,32]{0,1:T(8,128)S(1)}, s32[]{:T(128)}, s32[]{:T(128)}, /*index=5*/s32[]{:T(128)}) %tuple.711), condition=%wide.region_27.28_spmd.clone, body=%wide.region_26.27_spmd.clone.sunk | while | flops 2211 | bytes 10993 | solution.py:57
  698.2 45.1 %while.285 = (s32[]{:T(128)}, f32[32,32]{1,0:T(8,128)S(1)}, f32[32,32]{1,0:T(8,128)S(1)}, f32[32,32]{1,0:T(8,128)S(1)}, s32[]{:T(128)}, /*index=5*/s32[]{:T(128)}, s32[]{:T(128)}) while((s32[]{:T(128)}, f32[32,32]{1,0:T(8,128)S(1)}, f32[32,32]{1,0:T(8,128)S(1)}, f32[32,32]{1,0:T(8,128)S(1)}, s32[]{:T(128)}, /*index=5*/s32[]{:T(128)}, ...), condition=%wide.region_29.30_spmd, body=%wide.region_28.29_spmd.sunk | while | flops 12355 | bytes 19437 | solution.py:72
  745.4 45.5 %while.294 = (s32[]{:T(128)}, f32[32,32]{0,1:T(8,128)S(1)}, f32[32,32]{0,1:T(8,128)S(1)}, s32[]{:T(128)}, s32[]{:T(128)}, /*index=5*/s32[]{:T(128)}) while((s32[]{:T(128)}, f32[32,32]{0,1:T(8,128)S(1)}, f32[32,32]{0,1:T(8,128)S(1)}, s32[]{:T(128)}, s32[]{:T(128)}, /*index=5*/s32[]{:T(128)}) %tuple.717), condition=%wide.region_31.32_spmd.clone, body=%wide.region_30.31_spmd.clone.sunk | while | flops 2211 | bytes 10993 | solution.py:57
  791.0 45.1 %while.286 = (s32[]{:T(128)}, f32[32,32]{1,0:T(8,128)S(1)}, f32[32,32]{1,0:T(8,128)S(1)}, f32[32,32]{1,0:T(8,128)S(1)}, s32[]{:T(128)}, /*index=5*/s32[]{:T(128)}, s32[]{:T(128)}) while((s32[]{:T(128)}, f32[32,32]{1,0:T(8,128)S(1)}, f32[32,32]{1,0:T(8,128)S(1)}, f32[32,32]{1,0:T(8,128)S(1)}, s32[]{:T(128)}, /*index=5*/s32[]{:T(128)}, ...), condition=%wide.region_33.34_spmd, body=%wide.region_32.33_spmd.sunk | while | flops 12355 | bytes 19437 | solution.py:72
  841.6 45.6 %while.295 = (s32[]{:T(128)}, f32[32,32]{0,1:T(8,128)S(1)}, f32[32,32]{0,1:T(8,128)S(1)}, s32[]{:T(128)}, s32[]{:T(128)}, /*index=5*/s32[]{:T(128)}) while((s32[]{:T(128)}, f32[32,32]{0,1:T(8,128)S(1)}, f32[32,32]{0,1:T(8,128)S(1)}, s32[]{:T(128)}, s32[]{:T(128)}, /*index=5*/s32[]{:T(128)}) %tuple.723), condition=%wide.region_35.36_spmd.clone, body=%wide.region_34.35_spmd.clone.sunk | while | flops 2211 | bytes 10993 | solution.py:57
  887.2 45.1 %while.287 = (s32[]{:T(128)}, f32[32,32]{1,0:T(8,128)S(1)}, f32[32,32]{1,0:T(8,128)S(1)}, f32[32,32]{1,0:T(8,128)S(1)}, s32[]{:T(128)}, /*index=5*/s32[]{:T(128)}, s32[]{:T(128)}) while((s32[]{:T(128)}, f32[32,32]{1,0:T(8,128)S(1)}, f32[32,32]{1,0:T(8,128)S(1)}, f32[32,32]{1,0:T(8,128)S(1)}, s32[]{:T(128)}, /*index=5*/s32[]{:T(128)}, ...), condition=%wide.region_37.38_spmd, body=%wide.region_36.37_spmd.sunk | while | flops 12355 | bytes 19437 | solution.py:72
  934.5 0.8 bitcast_reduce_fusion.4
  938.5 0.8 bitcast_reduce_fusion.1
  947.8 2.8 fusion.48
  (2271 shorter events, 550.2 us)
Async XLA Ops:
  7.2 1.6 copy-start
  7.2 162.9 %all-gather.3.cloned.1.call-start = ((), (), s32[]{:S(2)}) async-start(), calls=%async_computation.2 | async-start | bytes 33816576 | tf_op jit(solution)/shard_map/all_gather | solution.py:14
  59.6 3.5 copy-start.1
  63.0 2.2 copy-start.2
  63.1 2.7 copy-start.3
  66.4 10.8 %all-to-all-start.1 = ((f32[32,1,8]{2,1,0:T(1,128)}), f32[32,1,8]{2,1,0:T(1,128)S(1)}, u32[]{:S(2)}, u32[]{:S(2)}) async-start(f32[32,1,8]{2,1,0:T(1,128)} %broadcast_in_dim.126), calls=%async_computation.1 | async-start | bytes 32768 | tf_op jit(solution)/shard_map/all_to_all | solution.py:28
Sparse Core Ops, SparseCore 0:
  65.3 104.7 all-gather.2
